TPU v7x, 512 devices: a whole 4x4x16 slice. The times are simulated.
512 devices in a mesh: seq: 32 (over y, z_lo), mp: 16 (over x, z_hi, core).
Axes of the slice: x: 4, y: 4, z: 16 (z_hi: 2, z_lo: 8; z = z_hi * 8 + z_lo), core: 2. Of those that a mesh axis runs over, the one named last changes fastest.
Arguments:
- tokens: bfloat16 [4096, 8192], P('seq', 'mp'), may hold values from -6 to 6
- in_weight: bfloat16 [8192, 3, 4096], P('seq', None, 'mp'), may hold values from -0.0625 to 0.0625
- short_taps: float32 [3, 3, 4096], P(None, None, 'mp'), may hold values from -4 to 4
- carry_rows: bfloat16 [2, 3, 4096], P(None, None, 'mp'), may hold values from -6 to 6
- pole_rates: float32 [16, 16], replicated, may hold values from 3e-05 to 0.03
- residues: float32 [16, 16], replicated, may hold values from -0.1 to 0.1
- carry_state: float32 [4096, 16], P('mp'), may hold values from -60 to 60
- skip_gain: float32 [4096], P('mp'), may hold values from -4 to 4
- groups: int32 [4096], P('mp'), may hold values from 0 to 15
Outputs:
- result: bfloat16 [4096, 4096], P('seq', 'mp')
All inputs are finite; a program needn't handle non-finite values.
Results may differ from a plain program's by a relative error of at most 0.008.
Values may be sent and summed in bfloat16 or wider, within the bound.
A program may use at most 128 MiB of HBM per device.

v0:
```python
import math
import jax
import jax.numpy as jnp
from jax import lax
from jax.sharding import PartitionSpec as P


def shifted(array, axis, by):
    length = lax.axis_size(axis)
    pairs = [(i, i + by) for i in range(length) if 0 <= i + by < length]
    return lax.ppermute(array, axis, pairs)


def project_rows(source, in_weight, out_width):
    gathered = lax.all_gather(source, "mp", axis=1, tiled=True)
    segment = lax.all_gather(in_weight, "seq", axis=0, tiled=True)
    return jnp.dot(
        gathered, segment.reshape(segment.shape[0], out_width), preferred_element_type=jnp.float32
    )


def channel_modes(chan_groups, pole_rates, residues):
    highest = lax.Precision.HIGHEST
    one_hot = (
        chan_groups[:, None] == jnp.arange(pole_rates.shape[0], dtype=jnp.int32)[None, :]
    ).astype(jnp.float32)
    chan_rates = jnp.dot(one_hot, pole_rates, precision=highest)
    chan_res = jnp.dot(one_hot, residues, precision=highest)
    return (chan_rates, chan_res)


def long_conv(signal, chan_rates, chan_res, chan_state, block_limit):
    highest = lax.Precision.HIGHEST
    chan_count, length = signal.shape
    block_len = math.gcd(length, block_limit)
    block_count = length // block_len
    steps_in = jnp.arange(block_len).astype(jnp.float32)
    decays = jnp.exp(-chan_rates[:, :, None] * steps_in)
    kernel = jnp.sum(chan_res[:, :, None] * decays, axis=1)
    lag_index = jnp.arange(block_len)[:, None] - jnp.arange(block_len)[None, :]
    toeplitz = jnp.where(lag_index >= 0, jnp.take(kernel, jnp.maximum(lag_index, 0), axis=1), 0.0)
    pieces = signal.reshape(chan_count, block_count, block_len)
    inner_part = jnp.einsum("cij,cnj->cni", toeplitz, pieces, precision=highest)
    tail_decay = jnp.exp(-chan_rates[:, :, None] * (block_len - 1.0 - steps_in))
    block_sums = jnp.einsum("crj,cnj->crn", tail_decay, pieces, precision=highest)
    index_blocks = jnp.arange(block_count)
    gap_steps = index_blocks[:, None] - 1 - index_blocks[None, :]
    gap_float = jnp.maximum(gap_steps, 0).astype(jnp.float32) * block_len
    transfer = jnp.where(gap_steps >= 0, jnp.exp(-chan_rates[:, :, None, None] * gap_float), 0.0)
    states = jnp.einsum("crnm,crm->crn", transfer, block_sums, precision=highest)
    start_decay = jnp.exp(-chan_rates[:, :, None] * (index_blocks.astype(jnp.float32) * block_len))
    states = states + start_decay * chan_state[:, :, None]
    lead_decay = chan_res[:, :, None] * jnp.exp(-chan_rates[:, :, None] * (steps_in + 1.0))
    outer_part = jnp.einsum("cri,crn->cni", lead_decay, states, precision=highest)
    return (inner_part + outer_part).reshape(chan_count, length)


def shards(
    tokens, in_weight, short_taps, carry_rows, pole_rates, residues, carry_state, skip_gain, groups
):
    row_count = tokens.shape[0]
    local_width = in_weight.shape[2]
    out_width = 3 * local_width
    is_first = lax.axis_index("seq") == 0
    projected = (
        project_rows(tokens, in_weight, out_width)
        .astype(jnp.bfloat16)
        .reshape(tokens.shape[0], 3, local_width)
    )
    head_rows = shifted(projected[row_count - 2 :], "seq", 1)
    head_rows = jnp.where(is_first, carry_rows, head_rows)
    extended = jnp.concatenate([head_rows, projected], axis=0).astype(jnp.float32)
    short_mix = (
        short_taps[0] * extended[2:]
        + short_taps[1] * extended[1:-1]
        + short_taps[2] * extended[:-2]
    )
    query_rows = short_mix[:, 0]
    gated_rows = (short_mix[:, 1] * short_mix[:, 2]).astype(jnp.bfloat16)
    channel_major = lax.all_to_all(gated_rows.T, "seq", split_axis=0, concat_axis=1, tiled=True)
    chan_count = channel_major.shape[0]
    offset = lax.axis_index("seq") * chan_count
    chan_groups = lax.dynamic_slice_in_dim(groups, offset, chan_count, 0)
    chan_state = lax.dynamic_slice_in_dim(carry_state, offset, chan_count, 0)
    chan_rates, chan_res = channel_modes(chan_groups, pole_rates, residues)
    long_mixed = long_conv(channel_major.astype(jnp.float32), chan_rates, chan_res, chan_state, 256)
    long_rows = lax.all_to_all(
        long_mixed.astype(jnp.bfloat16), "seq", split_axis=1, concat_axis=0, tiled=True
    ).T
    result = query_rows * (
        long_rows.astype(jnp.float32) + skip_gain * gated_rows.astype(jnp.float32)
    )
    return result.astype(jnp.bfloat16)


def solution(mesh):
    in_specs = (
        P("seq", "mp"),
        P("seq", None, "mp"),
        P(None, None, "mp"),
        P(None, None, "mp"),
        P(),
        P(),
        P("mp", None),
        P("mp"),
        P("mp"),
    )
    out_specs = P("seq", "mp")
    return jax.shard_map(shards, mesh=mesh, in_specs=in_specs, out_specs=out_specs, check_vma=False)
```

profile of v0, /device:TPU:4, one launch (start us, length us, event | category | flops | bytes accessed | tf_op | source)
XLA Modules:
  0.0 721.7 jit_solution(1981509274140765477)
XLA Ops:
  6.6 0.7 all-gather.3.cloned.1.call-update
  7.3 1.9 copy.25
  9.3 0.1 copy.37
  9.5 0.1 dynamic_slice.6
  9.6 0.1 constant_dynamic-slice_fusion
  9.7 0.2 convolution_negate_fusion
  9.9 0.2 fusion.41
  10.1 0.1 multiply_reduce_fusion
  10.2 0.1 fusion.40
  10.4 93.1 %all-gather.3.cloned.1.call-done = bf16[128,8192]{1,0:T(8,128)(2,1)} async-done(((bf16[128,512]{1,0:T(8,128)(2,1)}), bf16[128,8192]{1,0:T(8,128)(2,1)}) %all-gather.3.cloned.1.call-update) | async-done | bytes 2097168 | tf_op jit(solution)/shard_map/all_gather | solution.py:15
  103.5 316.7 %all-gather.5.cloned.1.call-done = bf16[8192,3,256]{0,2,1:T(8,128)(2,1)} async-done(((bf16[256,3,256]{0,2,1:T(8,128)(2,1)}), bf16[8192,3,256]{0,2,1:T(8,128)(2,1)}) %all-gather.5.cloned.1.call-update) | async-done | bytes 12582928 | tf_op jit(solution)/shard_map/all_gather | solution.py:16
  420.2 9.5 %convolution_convert_fusion = bf16[128,768]{1,0:T(8,128)(2,1)S(1)} fusion(bf16[128,8192]{1,0:T(8,128)(2,1)} %all-gather.3.cloned.1.call-done, bf16[8192,768]{0,1:T(8,128)(2,1)} %bitcast.52), kind=kOutput, calls=%fused_computation.5 | convolution fusion | flops 1610711040 | bytes 14876672 | tf_op jit(solution)/shard_map/dot_general | solution.py:17
  429.7 1.3 collective-permute-start
  431.0 0.2 copy.27
  431.2 1.1 collective-permute-done
  432.3 0.2 copy.28
  432.5 0.2 maximum_convert_fusion
  432.7 0.6 fusion.17
  433.3 0.6 fusion.56
  433.9 16.6 %all-to-all-start = ((bf16[32,8,128]{2,1,0:T(8,128)(2,1)}), bf16[32,8,128]{2,1,0:T(8,128)(2,1)S(1)}, u32[]{:S(2)}, u32[]{:S(2)}) async-start(bf16[32,8,128]{2,1,0:T(8,128)(2,1)} %fusion.56), calls=%async_computation | async-start | bytes 131072 | tf_op jit(solution)/shard_map/all_to_all | solution.py:80
  450.5 0.1 copy.30
  450.6 215.6 %gather_fusion = f32[65536,8]{1,0:T(8,128)} fusion(f32[8,256]{0,1:T(8,128)S(1)} %copy.30, s32[65536]{0:T(1024)S(1)} %broadcast_clamp_fusion), kind=kCustom, calls=%fused_computation | custom fusion | bytes 4456448 | tf_op jit(solution)/shard_map/jit(_take)/gather | solution.py:41
  666.3 18.6 %copy.31 = f32[256,256,8]{1,0,2:T(8,128)S(1)} copy(f32[256,256,8]{2,1,0:T(8,128)} %bitcast.51) | data formatting | bytes 4194304 | tf_op jit(solution)/shard_map/jit(_take)/gather | solution.py:41
  684.9 0.1 convert_multiply_fusion
  685.1 0.3 fusion.26
  685.4 1.9 fusion.7
  687.3 0.1 copy.36
  687.4 1.3 fusion
  688.7 0.3 fusion.4
  689.1 24.9 %all_to_all.26 = bf16[8,32,128]{2,0,1:T(8,128)(2,1)S(1)} all-to-all(bf16[8,32,128]{2,0,1:T(8,128)(2,1)S(1)} %copy.33), channel_id=1, replica_groups=mesh['seq'=32,'mp'=16] {'seq'}, dimensions={1} | all-to-all | bytes 131072 | tf_op jit(solution)/shard_map/all_to_all | solution.py:87
  714.0 0.1 fusion.22
  714.1 0.7 copy.34
  (35 shorter events, 0.5 us)
Async XLA Ops:
  6.5 3.0 copy-start
  6.5 2.9 copy-start.6
  6.5 3.2 copy-start.4
  6.5 3.4 copy-start.5
  6.5 3.8 copy-start.1
  6.5 96.9 %all-gather.3.cloned.1.call-start = ((), (), s32[]{:S(2)}) async-start(), calls=%async_computation.2 | async-start | bytes 2228224 | tf_op jit(solution)/shard_map/all_gather | solution.py:15
  7.3 412.9 %all-gather.5.cloned.1.call-start = ((), (), s32[]{:S(2)}) async-start(), calls=%async_computation.3 | async-start | bytes 12976128 | tf_op jit(solution)/shard_map/all_gather | solution.py:16
  420.2 12.1 %copy-start.2 = (bf16[2,3,256]{2,0,1:T(2,128)(2,1)S(1)}, bf16[2,3,256]{2,0,1:T(2,128)(2,1)}, u32[]{:S(2)}) copy-start(bf16[2,3,256]{2,0,1:T(2,128)(2,1)} %param.12) | copy-start | bytes 9220
  429.7 2.6 collective-permute-start
  433.9 251.1 %all-to-all-start = ((bf16[32,8,128]{2,1,0:T(8,128)(2,1)}), bf16[32,8,128]{2,1,0:T(8,128)(2,1)S(1)}, u32[]{:S(2)}, u32[]{:S(2)}) async-start(bf16[32,8,128]{2,1,0:T(8,128)(2,1)} %fusion.56), calls=%async_computation | async-start | bytes 131072 | tf_op jit(solution)/shard_map/all_to_all | solution.py:80
  685.3 28.7 %copy-start.3 = (f32[256]{0:T(256)S(1)}, f32[256]{0:T(256)}, u32[]{:S(2)}) copy-start(f32[256]{0:T(256)} %param.16) | copy-start | bytes 3076
Sparse Core Ops, SparseCore 0:
  10.5 92.9 all-gather.2
  105.5 314.6 all-gather.4
where the time goes:
time: 722 us
  waiting for transfers between devices  412 us (57%)
  local copies, waits for them, and re-layouts  238 us (33%)
  blocking collectives  24.9 us (3%)
  starting transfers between devices  17.9 us (2%)
  matrix products  13.7 us (2%)
  between operations  13.6 us (2%)
    all_gather x1, waiting for transfers between devices, project_rows(): segment = lax.all_gather(in_weight, 'seq', axis=0, tiled=True)  317 us
    gather x2, local copies, waits for them, and re-layouts, long_conv(): jnp.take(kernel, jnp.maximum(lag_index, 0), axis=1)  234 us
    all_gather x1, waiting for transfers between devices, project_rows(): gathered = lax.all_gather(source, 'mp', axis=1, tiled=True)  93.1 us
    all_to_all x1, blocking collectives, shards(): lax.all_to_all(long_mixed.astype(jnp.bfloat16), 'seq', split_axis=1, conc...  24.9 us
    all_to_all x1, starting transfers between devices, shards(): lax.all_to_all(gated_rows.T, 'seq', split_axis=0, concat_axis=1, tiled=True)  16.6 us
  transfers between devices with their start and end apart: 4, of which 3 were waited for; matrix products, arithmetic and copies ran while one was open for 33% of the time, Pallas kernels for 0%

commit v1 on v0

--- a/solution.py
+++ b/solution.py
@@ -3,6 +3,13 @@
 import jax.numpy as jnp
 from jax import lax
 from jax.sharding import PartitionSpec as P
+
+
+def exchange_gather(x, mesh_axis, d):
+    size = lax.axis_size(mesh_axis)
+    blocks = jnp.stack([x for _ in range(size)])
+    blocks = lax.all_to_all(blocks, mesh_axis, split_axis=0, concat_axis=0)
+    return jnp.concatenate(blocks, axis=d)
 
 
 def shifted(array, axis, by):
@@ -13,7 +20,7 @@
 
 def project_rows(source, in_weight, out_width):
     gathered = lax.all_gather(source, "mp", axis=1, tiled=True)
-    segment = lax.all_gather(in_weight, "seq", axis=0, tiled=True)
+    segment = exchange_gather(in_weight, "seq", 0)
     return jnp.dot(
         gathered, segment.reshape(segment.shape[0], out_width), preferred_element_type=jnp.float32
     )

time: 722 us -> 943 us (1.31)
  the two profiles are of different devices: /device:TPU:4 before, /device:TPU:6 now
where the time goes in v1:
time: 943 us; the launch traced here: 942 us
  waiting for transfers between devices  554 us (59%)
  local copies, waits for them, and re-layouts  266 us (28%)
  starting transfers between devices  68.5 us (7%)
  blocking collectives  24.8 us (3%)
  matrix products  13.7 us (1%)
  between operations  13.7 us (1%)
    all_to_all x1, waiting for transfers between devices, exchange_gather(): blocks = lax.all_to_all(blocks, mesh_axis, split_axis=0, concat_axis=0)  552 us
    gather x2, local copies, waits for them, and re-layouts, long_conv(): jnp.take(kernel, jnp.maximum(lag_index, 0), axis=1)  234 us
    ppermute x1, starting transfers between devices, shifted(): return lax.ppermute(array, axis, pairs)  34.9 us
    all_to_all x1, blocking collectives, shards(): lax.all_to_all(long_mixed.astype(jnp.bfloat16), 'seq', split_axis=1, conc...  24.8 us
  transfers between devices with their start and end apart: 4, of which 2 were waited for; matrix products, arithmetic and copies ran while one was open for 27% of the time, Pallas kernels for 0%

profile of v1, /device:TPU:6, one launch (start us, length us, event | category | flops | bytes accessed | tf_op | source)
XLA Modules:
  0.0 942.4 jit_solution(9719549452755626224)
XLA Ops:
  6.5 1.2 copy.26
  7.7 6.0 stack.2
  13.8 15.8 %all-to-all-start = ((bf16[32,256,3,256]{1,3,2,0:T(8,128)(2,1)}), bf16[32,256,3,256]{1,3,2,0:T(8,128)(2,1)}, u32[]{:S(2)}, u32[]{:S(2)}) async-start(bf16[32,256,3,256]{1,3,2,0:T(8,128)(2,1)} %stack.2), calls=%async_computation | async-start | bytes 25165824 | tf_op jit(solution)/shard_map/all_to_all | solution.py:11
  29.6 0.7 all-gather.2.cloned.1.call-update
  30.3 0.1 copy.40
  30.5 0.1 dynamic_slice.6
  30.6 0.1 constant_dynamic-slice_fusion
  30.7 0.2 convolution_negate_fusion
  30.9 0.2 fusion.41
  31.1 0.1 multiply_reduce_fusion
  31.4 552.1 %all-to-all-done = bf16[32,256,3,256]{1,3,2,0:T(8,128)(2,1)} async-done(((bf16[32,256,3,256]{1,3,2,0:T(8,128)(2,1)}), bf16[32,256,3,256]{1,3,2,0:T(8,128)(2,1)}, u32[]{:S(2)}, u32[]{:S(2)}) %all-to-all-start) | async-done | bytes 12582944 | tf_op jit(solution)/shard_map/all_to_all | solution.py:11
  583.5 11.9 %copy.27 = bf16[32,256,3,256]{1,0,3,2:T(8,128)(2,1)S(1)} copy(bf16[32,256,3,256]{1,3,2,0:T(8,128)(2,1)} %all-to-all-done) | data formatting | bytes 25165824 | tf_op jit(solution)/shard_map/all_to_all | solution.py:11
  595.4 10.7 %copy.39 = bf16[96,8,32,256]{3,1,2,0:T(8,128)(2,1)} copy(bf16[96,8,32,256]{3,2,1,0:T(8,128)(2,1)S(1)} %bitcast.56) | data formatting | bytes 25165824
  606.2 9.5 %convolution_convert_fusion = bf16[128,768]{1,0:T(8,128)(2,1)S(1)} fusion(bf16[128,8192]{1,0:T(8,128)(2,1)} %all-gather.2.cloned.1.call-done, bf16[8192,768]{0,1:T(8,128)(2,1)} %bitcast.55), kind=kOutput, calls=%fused_computation.5 | convolution fusion | flops 1610711040 | bytes 14876672 | tf_op jit(solution)/shard_map/dot_general | solution.py:24
  615.7 34.9 %collective-permute-start = (bf16[2,3,256]{2,1,0:T(4,128)(2,1)S(1)}, bf16[2,3,256]{2,1,0:T(4,128)(2,1)S(1)}, u32[]{:S(2)}, u32[]{:S(2)}) collective-permute-start(bf16[2,3,256]{2,1,0:T(4,128)(2,1)S(1)} %slice.35), channel_id=1, source_target_pairs={{0,16},{16,32},{32,48},{48,64},{64,80},{80,96},{96,112},{112,128},... | collective-permute-start | bytes 9224 | tf_op jit(solution)/shard_map/ppermute | solution.py:18
  650.6 0.2 copy.29
  650.8 1.1 collective-permute-done
  651.9 0.2 copy.30
  652.1 0.2 maximum_convert_fusion
  652.3 0.6 fusion.17
  652.9 0.6 fusion.56
  653.5 17.8 %all-to-all-start.1 = ((bf16[32,8,128]{2,1,0:T(8,128)(2,1)}), bf16[32,8,128]{2,1,0:T(8,128)(2,1)S(1)}, u32[]{:S(2)}, u32[]{:S(2)}) async-start(bf16[32,8,128]{2,1,0:T(8,128)(2,1)} %fusion.56), calls=%async_computation.1 | async-start | bytes 131072 | tf_op jit(solution)/shard_map/all_to_all | solution.py:87
  671.3 0.1 copy.32
  671.5 215.6 %gather_fusion = f32[65536,8]{1,0:T(8,128)} fusion(f32[8,256]{0,1:T(8,128)S(1)} %copy.32, s32[65536]{0:T(1024)S(1)} %broadcast_clamp_fusion), kind=kCustom, calls=%fused_computation | custom fusion | bytes 4456448 | tf_op jit(solution)/shard_map/jit(_take)/gather | solution.py:48
  887.1 18.6 %copy.33 = f32[256,256,8]{1,0,2:T(8,128)S(1)} copy(f32[256,256,8]{2,1,0:T(8,128)} %bitcast.57) | data formatting | bytes 4194304 | tf_op jit(solution)/shard_map/jit(_take)/gather | solution.py:48
  905.9 0.3 fusion.26
  906.2 1.9 fusion.7
  908.2 1.3 fusion
  909.5 0.3 fusion.4
  909.9 24.8 %all_to_all.31 = bf16[8,32,128]{2,0,1:T(8,128)(2,1)S(1)} all-to-all(bf16[8,32,128]{2,0,1:T(8,128)(2,1)S(1)} %copy.35), channel_id=1, replica_groups=mesh['seq'=32,'mp'=16] {'seq'}, dimensions={1} | all-to-all | bytes 131072 | tf_op jit(solution)/shard_map/all_to_all | solution.py:94
  934.7 0.1 fusion.22
  934.8 0.7 copy.36
  (39 shorter events, 0.6 us)
Async XLA Ops:
  6.5 24.1 %copy-start = (f32[256,16]{0,1:T(8,128)S(1)}, f32[256,16]{0,1:T(8,128)}, u32[]{:S(2)}) copy-start(f32[256,16]{0,1:T(8,128)} %param.15) | copy-start | bytes 49156
  13.7 16.7 %copy-start.7 = (s32[256]{0:T(256)S(1)}, s32[256]{0:T(256)}, u32[]{:S(2)}) copy-start(s32[256]{0:T(256)} %param.17) | copy-start | bytes 3076
  13.7 17.0 %copy-start.5 = (f32[16,16]{1,0:T(8,128)S(1)}, f32[16,16]{1,0:T(8,128)}, u32[]{:S(2)}) copy-start(f32[16,16]{1,0:T(8,128)} %param.13) | copy-start | bytes 3076
  13.7 17.2 %copy-start.6 = (f32[16,16]{1,0:T(8,128)S(1)}, f32[16,16]{1,0:T(8,128)}, u32[]{:S(2)}) copy-start(f32[16,16]{1,0:T(8,128)} %param.14) | copy-start | bytes 3076
  13.7 17.6 %copy-start.2 = (f32[3,3,256]{2,1,0:T(4,128)S(1)}, f32[3,3,256]{2,1,0:T(4,128)}, u32[]{:S(2)}) copy-start(f32[3,3,256]{2,1,0:T(4,128)} %param.11) | copy-start | bytes 27652
  13.8 569.8 %all-to-all-start = ((bf16[32,256,3,256]{1,3,2,0:T(8,128)(2,1)}), bf16[32,256,3,256]{1,3,2,0:T(8,128)(2,1)}, u32[]{:S(2)}, u32[]{:S(2)}) async-start(bf16[32,256,3,256]{1,3,2,0:T(8,128)(2,1)} %stack.2), calls=%async_computation | async-start | bytes 25165824 | tf_op jit(solution)/shard_map/all_to_all | solution.py:11
  29.6 576.6 %all-gather.2.cloned.1.call-start = ((), (), s32[]{:S(2)}) async-start(), calls=%async_computation.3 | async-start | bytes 2228224 | tf_op jit(solution)/shard_map/all_gather | solution.py:22
  606.2 45.8 %copy-start.3 = (bf16[2,3,256]{2,0,1:T(2,128)(2,1)S(1)}, bf16[2,3,256]{2,0,1:T(2,128)(2,1)}, u32[]{:S(2)}) copy-start(bf16[2,3,256]{2,0,1:T(2,128)(2,1)} %param.12) | copy-start | bytes 9220
  615.7 36.2 %collective-permute-start = (bf16[2,3,256]{2,1,0:T(4,128)(2,1)S(1)}, bf16[2,3,256]{2,1,0:T(4,128)(2,1)S(1)}, u32[]{:S(2)}, u32[]{:S(2)}) collective-permute-start(bf16[2,3,256]{2,1,0:T(4,128)(2,1)S(1)} %slice.35), channel_id=1, source_target_pairs={{0,16},{16,32},{32,48},{48,64},{64,80},{80,96},{96,112},{112,128},... | collective-permute-start | bytes 9224 | tf_op jit(solution)/shard_map/ppermute | solution.py:18
  653.5 252.3 %all-to-all-start.1 = ((bf16[32,8,128]{2,1,0:T(8,128)(2,1)}), bf16[32,8,128]{2,1,0:T(8,128)(2,1)S(1)}, u32[]{:S(2)}, u32[]{:S(2)}) async-start(bf16[32,8,128]{2,1,0:T(8,128)(2,1)} %fusion.56), calls=%async_computation.1 | async-start | bytes 131072 | tf_op jit(solution)/shard_map/all_to_all | solution.py:87
  906.2 28.5 %copy-start.4 = (f32[256]{0:T(256)S(1)}, f32[256]{0:T(256)}, u32[]{:S(2)}) copy-start(f32[256]{0:T(256)} %param.16) | copy-start | bytes 3076
  906.2 29.4 %copy-start.1 = (f32[256,16]{0,1:T(8,128)S(1)}, f32[256,16]{0,1:T(8,128)}, u32[]{:S(2)}) copy-start(f32[256,16]{0,1:T(8,128)} %param.15) | copy-start | bytes 49156
Sparse Core Ops, SparseCore 0:
  33.5 187.0 all-gather.1
